TPU v7x, 32 devices: a whole 2x2x4 slice. The times are simulated.
32 devices in a mesh: aux: 8 (over z, x), grp: 4 (over y, core).
Axes of the slice: x: 2, y: 2, z: 4, core: 2. Of those that a mesh axis runs over, the one named last changes fastest.
Arguments:
- source: float32 [1024, 256], P(('aux', 'grp')), may hold values from -6 to 6
- vir_energy: float32 [1024], P(('aux', 'grp')), may hold values from 0.5 to 3
- occ_energy: float32 [256], replicated, may hold values from -2 to -0.5
- factor_vv: float32 [64, 1024, 1024], P(('aux', 'grp')), may hold values from -0.375 to 0.375
- factor_oo: float32 [64, 256, 256], P(('aux', 'grp')), may hold values from -0.046875 to 0.046875
Outputs:
- response: float32 [1024, 256], P(('aux', 'grp'))
All inputs are finite; a program needn't handle non-finite values.
Results may differ from a plain program's by a relative error of at most 0.0001.
Values sent between devices are 32-bit elements; how exact they have to be, the bound alone decides.
A program may use at most 64 MiB of HBM per device.

v0:
```python
import jax
import jax.numpy as jnp
from jax import lax
from jax.sharding import PartitionSpec as P

ITERS = 2


def right_product(piece, factor_oo):
    return jnp.einsum(
        "bi,pij->pbj",
        piece,
        factor_oo,
        precision=lax.Precision.HIGHEST,
        preferred_element_type=jnp.float32,
    )


def left_product(factor_vv, halfway):
    return jnp.einsum(
        "pab,pbj->aj",
        factor_vv,
        halfway,
        precision=lax.Precision.HIGHEST,
        preferred_element_type=jnp.float32,
    )


def local(source, vir_energy, occ_energy, factor_vv, factor_oo):
    own_rows = source.shape[0]
    whole_source, whole_vir = (
        lax.all_gather(source, ("aux", "grp"), axis=0, tiled=True),
        lax.all_gather(vir_energy, ("aux", "grp"), axis=0, tiled=True),
    )
    whole_gap = whole_vir[:, None] - occ_energy[None, :]
    whole = whole_source / whole_gap
    for sweep in range(ITERS):
        terms = left_product(factor_vv, right_product(whole, factor_oo))
        summed = lax.psum(terms, ("aux", "grp"))
        whole = (whole_source - summed) / whole_gap
    offset = lax.axis_index(("aux", "grp")) * own_rows
    return lax.dynamic_slice_in_dim(whole, offset, own_rows, 0)


def solution(mesh):
    placed = (
        P(("aux", "grp"), None),
        P(("aux", "grp")),
        P(),
        P(("aux", "grp"), None, None),
        P(("aux", "grp"), None, None),
    )
    return jax.shard_map(
        local, mesh=mesh, in_specs=placed, out_specs=P(("aux", "grp"), None), check_vma=False
    )
```

profile of v0, /device:TPU:0, one launch (start us, length us, event | category | flops | bytes accessed | tf_op | source)
XLA Modules:
  0.0 368.5 jit_solution(17886522956416161345)
XLA Ops:
  6.5 0.0 copy-start
  6.5 0.0 copy-start.2
  6.5 0.0 all-gather.2.cloned.1.call-start
  6.5 0.7 all-gather.2.cloned.1.call-update
  7.3 0.0 all-reduce.4.cloned.1.call-start
  7.3 0.9 dynamic-update-slice
  8.2 42.0 %all-reduce = f32[1024]{0:T(1024)S(1)} all-reduce(f32[1024]{0:T(1024)S(1)} %dynamic-update-slice), channel_id=1, replica_groups=mesh['aux'=8,'grp'=4] {'aux','grp'}, use_global_device_ids=true, to_apply=%add | all-reduce | flops 1024 | bytes 8192
  50.2 16.5 %all-gather.2.cloned.1.call-done = f32[1024,256]{1,0:T(8,128)} async-done(((f32[32,256]{1,0:T(8,128)}), f32[1024,256]{1,0:T(8,128)}) %all-gather.2.cloned.1.call-update) | async-done | bytes 1048592 | tf_op jit(solution)/shard_map/all_gather | solution.py:32
  66.7 1.6 copy.10
  68.3 0.0 copy-done
  68.3 0.0 copy-done.2
  68.3 0.0 copy-start.1
  68.3 2.0 fusion.12
  70.3 1.6 copy.19
  72.0 0.0 copy-done.1
  72.0 14.8 %fusion.4 = f32[1024,256]{0,1:T(8,128)} fusion(f32[2,1024,1024]{2,1,0:T(8,128)S(1)} %copy-done.1, f32[2,1024,256]{2,0,1:T(2,128)S(1)} %bitcast.26), kind=kOutput, calls=%fused_computation.5 | convolution fusion | flops 6442450944 | bytes 11534336 | tf_op jit(solution)/shard_map/pab,pbj->aj/dot_general | solution.py:20
  86.7 0.0 all-reduce.4.cloned.1.call-update
  86.8 0.0 all-reduce.6.cloned.1.call-start
  86.8 129.7 %all-reduce.4.cloned.1.call-done = f32[1024,256]{0,1:T(8,128)} async-done(((f32[1024,256]{0,1:T(8,128)}), f32[1024,256]{0,1:T(8,128)}) %all-reduce.4.cloned.1.call-update) | async-done | bytes 1048592 | tf_op jit(solution)/shard_map/psum | solution.py:39
  216.5 3.4 fusion.10
  220.0 10.4 %fusion.7 = f32[1024,256]{0,1:T(8,128)} fusion(f32[2,1024,1024]{2,1,0:T(8,128)} %param.8, f32[1024,2,256]{0,2,1:T(8,128)S(1)} %fusion.10), kind=kOutput, calls=%fused_computation.6 | convolution fusion | flops 6442450944 | bytes 11534336 | tf_op jit(solution)/shard_map/pab,pbj->aj/dot_general | solution.py:20
  230.4 0.0 all-reduce.6.cloned.1.call-update
  230.4 0.1 broadcast_subtract_fusion
  230.5 129.6 %all-reduce.6.cloned.1.call-done = f32[1024,256]{0,1:T(8,128)} async-done(((f32[1024,256]{0,1:T(8,128)}), f32[1024,256]{0,1:T(8,128)}) %all-reduce.6.cloned.1.call-update) | async-done | bytes 1048592 | tf_op jit(solution)/shard_map/psum | solution.py:39
  360.2 1.1 dynamic-slice_divide_fusion
  361.3 0.7 copy.11
  (1 shorter events, 0.0 us)
Async XLA Ops:
  6.5 61.8 %copy-start = (f32[2,256,256]{2,1,0:T(8,128)S(1)}, f32[2,256,256]{2,1,0:T(8,128)}, u32[]{:S(2)}) copy-start(f32[2,256,256]{2,1,0:T(8,128)} %param.9) | copy-start | bytes 1572868
  6.5 61.8 %copy-start.2 = (f32[256]{0:T(256)S(1)}, f32[256]{0:T(256)}, u32[]{:S(2)}) copy-start(f32[256]{0:T(256)} %param.7) | copy-start | bytes 3076
  6.5 60.2 %all-gather.2.cloned.1.call-start = ((), (), s32[]{:S(2)}) async-start(), calls=%async_computation | async-start | bytes 1081344 | tf_op jit(solution)/shard_map/all_gather | solution.py:32
  7.3 209.3 %all-reduce.4.cloned.1.call-start = ((), (), s32[]{:S(2)}) async-start(), calls=%async_computation.1 | async-start | bytes 2097152 | tf_op jit(solution)/shard_map/psum | solution.py:39
  68.3 3.7 copy-start.1
  86.8 273.4 %all-reduce.6.cloned.1.call-start = ((), (), s32[]{:S(2)}) async-start(), calls=%async_computation.2 | async-start | bytes 2097152 | tf_op jit(solution)/shard_map/psum | solution.py:39
Sparse Core Ops, SparseCore 0:
  10.2 56.4 all-gather.1
  86.9 129.6 all-reduce.3
  230.5 129.6 all-reduce.5
where the time goes:
time: 369 us; the launch traced here: 368 us
  waiting for transfers between devices  277 us (75%)
  blocking collectives  42 us (11%)
  matrix products  30.6 us (8%)
  between operations  13.2 us (4%)
  local copies, waits for them, and re-layouts  4.74 us (1%)
    psum x2, waiting for transfers between devices, local(): summed = lax.psum(terms, ('aux', 'grp'))  259 us
    unnamed x1, blocking collectives  42 us
    dot_general x2, matrix products, left_product(): jnp.einsum('pab,pbj->aj', factor_vv, halfway, precision=lax.Precision.HIG...  25.2 us
    all_gather x1, waiting for transfers between devices, local(): lax.all_gather(source, ('aux', 'grp'), axis=0, tiled=True)  16.5 us
  transfers between devices with their start and end apart: 3, of which 3 were waited for; matrix products, arithmetic and copies ran while one was open for 0% of the time, Pallas kernels for 0%

commit v1 on v0

v1 whole, which is shorter than its diff:
```python
import functools

import jax
import jax.numpy as jnp
from jax import lax
from jax.experimental import pallas as pl
from jax.experimental.pallas import tpu as pltpu
from jax.sharding import PartitionSpec as P

ITERS = 2
AXES = ("aux", "grp")
F32 = jnp.float32
BF16 = jnp.bfloat16
MESH = pl.DeviceIdType.MESH
GROUPS = 4
HALVES = 2


def split(value):
    high = value.astype(BF16)
    return high, (value - high.astype(F32)).astype(BF16)


def dot3(a, b):
    (ah, al), (bh, bl) = a, b
    dot = functools.partial(jnp.dot, preferred_element_type=F32)
    return dot(ah, bh) + (dot(ah, bl) + dot(al, bh))


def kernel(
    sizes, source, vir, occ, oo, vv, out,
    stage, vh, vl, oh, ol, th, tl, acc, gathered, from_partner, received,
    load_sem, gather_send, gather_recv, pair_send, pair_recv, scatter_send, scatter_recv,
):
    naux, ngrp, rows = sizes
    chips, pairs = naux * ngrp // 2, ngrp // 2
    terms, width = oo.shape[0], oo.shape[1]
    per_group = chips // GROUPS
    span = 2 * per_group * rows
    per_half = chips // HALVES
    tall = per_half * rows
    aux, grp = lax.axis_index("aux"), lax.axis_index("grp")
    core = grp % 2
    chip = aux * pairs + grp // 2

    def device(which, side):
        return (which // pairs, (which % pairs) * 2 + side)

    partner = device(chip, 1 - core)

    loads = []
    for slot in range(2):
        side = (1 - core) if slot == 0 else core
        for p in range(terms):
            load = pltpu.make_async_copy(vv.at[p, :, side], stage.at[slot, p], load_sem.at[slot, p])
            load.start()
            loads.append(load)

    barrier = pltpu.get_barrier_semaphore()
    pl.semaphore_signal(barrier, inc=1, device_id=partner, device_id_type=MESH)
    for o in range(1, chips):
        pl.semaphore_signal(
            barrier, inc=1, device_id=device((chip + o) % chips, core), device_id_type=MESH
        )

    at_row = lax.broadcasted_iota(jnp.int32, (rows, rows), 0)
    at_column = lax.broadcasted_iota(jnp.int32, (rows, rows), 1)
    spread = jnp.broadcast_to(vir[...], (rows, rows))
    vir_column = jnp.sum(jnp.where(at_row == at_column, spread, 0.0), axis=1, keepdims=True)
    gap = vir_column - occ[...]
    mine = source[...] / gap
    own = 2 * chip + core
    gathered[0, own] = mine
    for p in range(terms):
        oh[p], ol[p] = split(oo[p])
    pl.semaphore_wait(barrier, chips)

    home = chip // per_group
    inside = chip % per_group
    order = [(home + g) % GROUPS for g in (0, 1, 3, 2)]

    def peers(g):
        start = order[g] * per_group
        return [start + (inside + o) % per_group for o in range(1 if g == 0 else 0, per_group)]

    def gather_to_partner(it, block):
        return pltpu.make_async_remote_copy(
            gathered.at[it, block], gathered.at[it, block],
            gather_send.at[it, 1, block // 2], gather_recv.at[it, block],
            device_id=partner, device_id_type=MESH,
        )

    def gather_to(it, other):
        return pltpu.make_async_remote_copy(
            gathered.at[it, own], gathered.at[it, own],
            gather_send.at[it, 0, other], gather_recv.at[it, own],
            device_id=device(other, core), device_id_type=MESH,
        )

    def arrival(it, block):
        return pltpu.make_async_remote_copy(
            gathered.at[it, block], gathered.at[it, block],
            gather_send.at[it, 1, block // 2], gather_recv.at[it, block],
            device_id=partner, device_id_type=MESH,
        )

    def start_gather(it):
        sends = []
        for g in (1, 2, 0, 3):
            for other in peers(g):
                sends.append(gather_to(it, other))
                sends[-1].start()
        sends.append(gather_to_partner(it, own))
        sends[-1].start()
        return sends

    def product(q, slot, at):
        place = pl.ds(pl.multiple_of(at * tall, tall), tall)
        total = None
        for p in range(terms):
            term = dot3(
                (vh[q, p, slot, place, :], vl[q, p, slot, place, :]), (th[p], tl[p])
            )
            total = term if total is None else total + term
        return total

    def halfway(it, q):
        piece = gathered[it, pl.ds(q * 2 * per_group, 2 * per_group)].reshape(span, width)
        piece = split(piece)
        for p in range(terms):
            th[p], tl[p] = split(dot3(piece, (oh[p], ol[p])))

    sends = start_gather(0)

    for slot in range(2):
        for p in range(terms):
            loads[slot * terms + p].wait()

            def convert(c, carry):
                value = stage[slot, p, c]
                high, low = split(value)
                place = pl.ds(pl.multiple_of(c * rows, rows), rows)
                for q in range(GROUPS):
                    vh[q, p, slot, place, :] = high[:, q * span:(q + 1) * span]
                    vl[q, p, slot, place, :] = low[:, q * span:(q + 1) * span]
                return carry

            lax.fori_loop(0, chips, convert, 0)

    near = chip // per_half
    far = (near + 1) % HALVES
    within = chip % per_half

    for it in range(ITERS):
        def consume(g):
            q = order[g]
            for other in ([chip] if g == 0 else []) + peers(g):
                arrival(it, 2 * other + 1 - core).wait_recv()
            halfway(it, q)
            return q

        def accumulate(g):
            q = consume(g)

            def step(i, carry):
                slot, at = i // HALVES, i % HALVES
                place = pl.ds(pl.multiple_of(at * tall, tall), tall)
                term = product(q, slot, at)
                if g == 0:
                    acc[slot, place, :] = term
                else:
                    acc[slot, place, :] += term
                return carry

            lax.fori_loop(0, 2 * HALVES, step, 0)

        for g in range(GROUPS):
            for other in peers(g):
                arrival(it, 2 * other + core).wait_recv()
                sends.append(gather_to_partner(it, 2 * other + core))
                sends[-1].start()
            if g > 0:
                accumulate(g - 1)

        q = consume(GROUPS - 1)
        handed = []
        for at in (far, near):
            place = pl.ds(pl.multiple_of(at * tall, tall), tall)
            acc[0, place, :] += product(q, 0, at)
            handed.append(pltpu.make_async_remote_copy(
                acc.at[0, place], from_partner.at[it, at],
                pair_send.at[it, at], pair_recv.at[it, at],
                device_id=partner, device_id_type=MESH,
            ))
            handed[-1].start()

        def scatter_to(other, sender):
            return pltpu.make_async_remote_copy(
                acc.at[1, pl.ds(pl.multiple_of(other * rows, rows), rows)],
                received.at[it, sender],
                scatter_send.at[it, other], scatter_recv.at[it, sender],
                device_id=device(other, core), device_id_type=MESH,
            )

        scattered = []
        others = []
        for n, at in enumerate((far, near)):
            place = pl.ds(pl.multiple_of(at * tall, tall), tall)
            term = product(q, 1, at)
            handed[n].wait_recv()
            acc[1, place, :] += term + from_partner[it, at]
            for o in range(n, per_half):
                other = at * per_half + (within + o) % per_half
                others.append(other)
                scattered.append(scatter_to(other, chip))
                scattered[-1].start()
        summed = acc[1, pl.ds(pl.multiple_of(chip * rows, rows), rows), :]
        for other in others[per_half:] + others[:per_half]:
            scatter_to(other, other).wait_recv()
            summed = summed + received[it, other]
        mine = (source[...] - summed) / gap
        if it + 1 < ITERS:
            gathered[it + 1, own] = mine
            later = start_gather(it + 1)
        else:
            out[...] = mine
            later = []
        for copy in sends + handed + scattered:
            copy.wait_send()
        sends = later


def fused(sizes, source, vir_energy, occ_energy, factor_vv, factor_oo):
    naux, ngrp = sizes
    rows, width = source.shape
    terms, whole, _ = factor_vv.shape
    chips = naux * ngrp // 2
    span = whole // GROUPS
    tall = chips // HALVES * rows
    vmem = pl.BlockSpec(memory_space=pltpu.VMEM)
    dma = pltpu.SemaphoreType.DMA
    return pl.pallas_call(
        functools.partial(kernel, (naux, ngrp, rows)),
        out_shape=jax.ShapeDtypeStruct((rows, width), F32),
        in_specs=[vmem] * 4 + [pl.BlockSpec(memory_space=pl.ANY)],
        out_specs=vmem,
        scratch_shapes=[
            pltpu.VMEM((2, terms, chips, rows, whole), F32),
            pltpu.VMEM((GROUPS, terms, 2, chips * rows, span), BF16),
            pltpu.VMEM((GROUPS, terms, 2, chips * rows, span), BF16),
            pltpu.VMEM((terms, width, width), BF16),
            pltpu.VMEM((terms, width, width), BF16),
            pltpu.VMEM((terms, span, width), BF16),
            pltpu.VMEM((terms, span, width), BF16),
            pltpu.VMEM((2, chips * rows, width), F32),
            pltpu.VMEM((ITERS, 2 * chips, rows, width), F32),
            pltpu.VMEM((ITERS, HALVES, tall, width), F32),
            pltpu.VMEM((ITERS, chips, rows, width), F32),
            dma((2, terms)),
            dma((ITERS, 2, chips)),
            dma((ITERS, 2 * chips)),
            dma((ITERS, HALVES)),
            dma((ITERS, HALVES)),
            dma((ITERS, chips)),
            dma((ITERS, chips)),
        ],
        compiler_params=pltpu.CompilerParams(collective_id=0, has_side_effects=True),
    )(
        source,
        vir_energy.reshape(1, rows),
        occ_energy.reshape(1, width),
        factor_oo,
        factor_vv.reshape(terms, chips, 2, rows, whole),
    )


def plain(source, vir_energy, occ_energy, factor_vv, factor_oo):
    gap = vir_energy[:, None] - occ_energy[None, :]
    einsum = functools.partial(
        jnp.einsum, precision=lax.Precision.HIGHEST, preferred_element_type=F32
    )
    mine = source / gap
    for _ in range(ITERS):
        whole = lax.all_gather(mine, AXES, axis=0, tiled=True)
        terms = einsum("pab,pbj->aj", factor_vv, einsum("bi,pij->pbj", whole, factor_oo))
        summed = lax.psum_scatter(terms, AXES, scatter_dimension=0, tiled=True)
        mine = (source - summed) / gap
    return mine


def local(sizes, source, *rest):
    chips = sizes[0] * sizes[1] // 2
    rows, width = source.shape
    whole = chips * 2 * rows
    fits = (
        rows % 16 == 0 and sizes[1] % 2 == 0 and GROUPS == 4 and chips % GROUPS == 0
        and HALVES == 2 and whole % (GROUPS * 128) == 0 and width % 128 == 0
    )
    return fused(sizes, source, *rest) if fits else plain(source, *rest)


def solution(mesh):
    sizes = (mesh.shape["aux"], mesh.shape["grp"])
    placed = (P(AXES, None), P(AXES), P(), P(AXES, None, None), P(AXES, None, None))
    return jax.shard_map(
        functools.partial(local, sizes),
        mesh=mesh, in_specs=placed, out_specs=P(AXES, None), check_vma=False,
    )
```

time: 369 us -> 76.6 us (0.21)
  waiting for transfers between devices: 277 us -> 0 us
  Pallas kernels: 0 us -> 75 us
  blocking collectives: 42 us -> 0 us
  matrix products: 30.6 us -> 0 us
  between operations: 13.2 us -> 0.01 us
    psum x2 -> x0, waiting for transfers between devices: 259 us -> none  [local(): summed = lax.psum(terms, ('aux', 'grp'))]
    pallas_call x0 -> x1, Pallas kernels: none -> 75 us  [fused(): pl.pallas_call(functools.partial(kernel, (naux, ngrp, rows)), out_shape=j...]
    unnamed x1 -> x0, blocking collectives: 42 us -> none
    dot_general x4 -> x0, matrix products: 30.6 us -> none  [the longest x2 25.2 us: left_product(): jnp.einsum('pab,pbj->aj', factor_vv, halfway, precision=lax.Precision.HIG...]
    all_gather x1 -> x0, waiting for transfers between devices: 16.5 us -> none  [local(): lax.all_gather(source, ('aux', 'grp'), axis=0, tiled=True)]
  transfers between devices with their start and end apart: 3 -> 0, of which waited for: 3 -> 0; matrix products, arithmetic and copies ran while one was open for 0% -> 0% of each run, Pallas kernels for 0% -> 0%
where the time goes in v1:
time: 76.6 us; the launch traced here: 76.4 us
  Pallas kernels  75 us (98%)
  local copies, waits for them, and re-layouts  1.38 us (2%)
    pallas_call x1, Pallas kernels, fused(): pl.pallas_call(functools.partial(kernel, (naux, ngrp, rows)), out_shape=j...  75 us

profile of v1, /device:TPU:0, one launch (start us, length us, event | category | flops | bytes accessed | tf_op | source)
XLA Modules:
  0.0 76.4 jit_solution(10255434863979221966)
XLA Ops:
  0.0 75.0 %shard_map.55 = f32[32,256]{1,0:T(8,128)} custom-call(f32[32,256]{1,0:T(8,128)} %source.1, f32[1,32]{1,0:T(1,128)} %bitcast.5, f32[1,256]{1,0:T(1,128)} %bitcast.4, f32[2,256,256]{2,1,0:T(8,128)} %oo.1, f32[2,16,2,32,1024]{4,3,2,1,0:T(8,128)} %bitcast.3), custom_call_target="tpu_custom_call" | custom-call | tf_op jit(solution)/shard_map/pallas_call | solution.py:242
  75.1 1.4 %copy.7 = f32[32,256]{1,0:T(8,128)} copy(f32[32,256]{1,0:T(8,128)} %shard_map.55) | data formatting | bytes 65536

commit v2 on v1

--- a/solution.py
+++ b/solution.py
@@ -46,7 +46,18 @@
     def device(which, side):
         return (which // pairs, (which % pairs) * 2 + side)
 
+    z, x, y = aux // 2, aux % 2, grp // 2
+
+    def column(dx, dy):
+        return ((x + dx) % 2) * 2 + (y + dy) % 2
+
+    self_, first, second, both = column(0, 0), column(1 - core, core), column(core, 1 - core), column(1, 1)
+
+    def at(plane, col):
+        return plane * 4 + col
+
     partner = device(chip, 1 - core)
+    to_first, to_second = device(at(z, first), core), device(at(z, second), core)
 
     loads = []
     for slot in range(2):
@@ -58,10 +69,10 @@
 
     barrier = pltpu.get_barrier_semaphore()
     pl.semaphore_signal(barrier, inc=1, device_id=partner, device_id_type=MESH)
-    for o in range(1, chips):
-        pl.semaphore_signal(
-            barrier, inc=1, device_id=device((chip + o) % chips, core), device_id_type=MESH
-        )
+    order = [z, z + 1 - 2 * (z % 2), 2 - z // 2, 3 - 3 * (z // 2)]
+    greeted = [to_first, to_second] + [device(at(plane, self_), core) for plane in order[1:]]
+    for other in greeted:
+        pl.semaphore_signal(barrier, inc=1, device_id=other, device_id_type=MESH)
 
     at_row = lax.broadcasted_iota(jnp.int32, (rows, rows), 0)
     at_column = lax.broadcasted_iota(jnp.int32, (rows, rows), 1)
@@ -73,49 +84,36 @@
     gathered[0, own] = mine
     for p in range(terms):
         oh[p], ol[p] = split(oo[p])
-    pl.semaphore_wait(barrier, chips)
-
-    home = chip // per_group
-    inside = chip % per_group
-    order = [(home + g) % GROUPS for g in (0, 1, 3, 2)]
-
-    def peers(g):
-        start = order[g] * per_group
-        return [start + (inside + o) % per_group for o in range(1 if g == 0 else 0, per_group)]
-
-    def gather_to_partner(it, block):
+    pl.semaphore_wait(barrier, 1 + len(greeted))
+
+    def remote(src, dst, send, recv, target):
         return pltpu.make_async_remote_copy(
-            gathered.at[it, block], gathered.at[it, block],
-            gather_send.at[it, 1, block // 2], gather_recv.at[it, block],
-            device_id=partner, device_id_type=MESH,
+            src, dst, send, recv, device_id=target, device_id_type=MESH
         )
 
-    def gather_to(it, other):
-        return pltpu.make_async_remote_copy(
-            gathered.at[it, own], gathered.at[it, own],
-            gather_send.at[it, 0, other], gather_recv.at[it, own],
-            device_id=device(other, core), device_id_type=MESH,
-        )
-
-    def arrival(it, block):
-        return pltpu.make_async_remote_copy(
-            gathered.at[it, block], gathered.at[it, block],
-            gather_send.at[it, 1, block // 2], gather_recv.at[it, block],
-            device_id=partner, device_id_type=MESH,
-        )
+    def block_copy(it, block, kind, index, target):
+        piece = gathered.at[it, block]
+        return remote(piece, piece, gather_send.at[it, kind, index], gather_recv.at[it, block], target)
+
+    def arrived(it, which, side):
+        block_copy(it, 2 * which + side, 0, which, partner).wait_recv()
+
+    def pass_on(it, which, sends, targets):
+        for kind, target in targets:
+            sends.append(block_copy(it, 2 * which + core, kind, which, target))
+            sends[-1].start()
 
     def start_gather(it):
         sends = []
-        for g in (1, 2, 0, 3):
-            for other in peers(g):
-                sends.append(gather_to(it, other))
-                sends[-1].start()
-        sends.append(gather_to_partner(it, own))
-        sends[-1].start()
+        for plane in order[1:]:
+            there = at(plane, self_)
+            sends.append(block_copy(it, own, 3, there, device(there, core)))
+            sends[-1].start()
+        pass_on(it, chip, sends, ((0, to_first), (1, to_second), (2, partner)))
         return sends
 
-    def product(q, slot, at):
-        place = pl.ds(pl.multiple_of(at * tall, tall), tall)
+    def product(q, slot, half):
+        place = pl.ds(pl.multiple_of(half * tall, tall), tall)
         total = None
         for p in range(terms):
             term = dot3(
@@ -149,23 +147,37 @@
 
     near = chip // per_half
     far = (near + 1) % HALVES
-    within = chip % per_half
 
     for it in range(ITERS):
+        def from_plane(g):
+            which = at(order[g], self_)
+            arrived(it, which, core)
+            pass_on(it, which, sends, ((0, to_first), (1, to_second), (2, partner)))
+
+        def from_first(g):
+            which = at(order[g], first)
+            arrived(it, which, core)
+            pass_on(it, which, sends, ((1, to_second), (2, partner)))
+
+        def from_second(g):
+            for col in (second, both):
+                which = at(order[g], col)
+                arrived(it, which, core)
+                pass_on(it, which, sends, ((2, partner),))
+
         def consume(g):
-            q = order[g]
-            for other in ([chip] if g == 0 else []) + peers(g):
-                arrival(it, 2 * other + 1 - core).wait_recv()
-            halfway(it, q)
-            return q
+            for col in (self_, first, second, both):
+                arrived(it, at(order[g], col), 1 - core)
+            halfway(it, order[g])
+            return order[g]
 
         def accumulate(g):
             q = consume(g)
 
             def step(i, carry):
-                slot, at = i // HALVES, i % HALVES
-                place = pl.ds(pl.multiple_of(at * tall, tall), tall)
-                term = product(q, slot, at)
+                slot, half = i // HALVES, i % HALVES
+                place = pl.ds(pl.multiple_of(half * tall, tall), tall)
+                term = product(q, slot, half)
                 if g == 0:
                     acc[slot, place, :] = term
                 else:
@@ -174,50 +186,75 @@
 
             lax.fori_loop(0, 2 * HALVES, step, 0)
 
-        for g in range(GROUPS):
-            for other in peers(g):
-                arrival(it, 2 * other + core).wait_recv()
-                sends.append(gather_to_partner(it, 2 * other + core))
-                sends[-1].start()
-            if g > 0:
-                accumulate(g - 1)
-
-        q = consume(GROUPS - 1)
-        handed = []
-        for at in (far, near):
-            place = pl.ds(pl.multiple_of(at * tall, tall), tall)
-            acc[0, place, :] += product(q, 0, at)
-            handed.append(pltpu.make_async_remote_copy(
-                acc.at[0, place], from_partner.at[it, at],
-                pair_send.at[it, at], pair_recv.at[it, at],
-                device_id=partner, device_id_type=MESH,
-            ))
-            handed[-1].start()
-
-        def scatter_to(other, sender):
-            return pltpu.make_async_remote_copy(
-                acc.at[1, pl.ds(pl.multiple_of(other * rows, rows), rows)],
-                received.at[it, sender],
-                scatter_send.at[it, other], scatter_recv.at[it, sender],
-                device_id=device(other, core), device_id_type=MESH,
+        from_plane(1)
+        from_first(0)
+        from_plane(2)
+        from_first(1)
+        from_second(0)
+        from_plane(3)
+        from_first(2)
+        accumulate(0)
+        from_first(3)
+        from_second(1)
+        accumulate(1)
+        from_second(2)
+        accumulate(2)
+        from_second(3)
+        q = consume(3)
+
+        def piece(which):
+            return pl.ds(pl.multiple_of(which * rows, rows), rows)
+
+        def scatter(stage_, plane, col, target):
+            which = at(plane, col)
+            return remote(
+                acc.at[1, piece(which)], received.at[it, stage_, which],
+                scatter_send.at[it, stage_, which], scatter_recv.at[it, stage_, which], target,
             )
 
-        scattered = []
-        others = []
-        for n, at in enumerate((far, near)):
-            place = pl.ds(pl.multiple_of(at * tall, tall), tall)
-            term = product(q, 1, at)
-            handed[n].wait_recv()
-            acc[1, place, :] += term + from_partner[it, at]
-            for o in range(n, per_half):
-                other = at * per_half + (within + o) % per_half
-                others.append(other)
-                scattered.append(scatter_to(other, chip))
-                scattered[-1].start()
-        summed = acc[1, pl.ds(pl.multiple_of(chip * rows, rows), rows), :]
-        for other in others[per_half:] + others[:per_half]:
-            scatter_to(other, other).wait_recv()
-            summed = summed + received[it, other]
+        def to_plane(plane, sender):
+            return remote(
+                acc.at[1, piece(at(plane, self_))], received.at[it, 2, sender],
+                scatter_send.at[it, 2, plane], scatter_recv.at[it, 2, sender],
+                device(at(plane, self_), core),
+            )
+
+        def begin(copy):
+            sends.append(copy)
+            copy.start()
+
+        for half in (far, near):
+            place = pl.ds(pl.multiple_of(half * tall, tall), tall)
+            acc[0, place, :] += product(q, 0, half)
+            handed = remote(
+                acc.at[0, place], from_partner.at[it, half],
+                pair_send.at[it, half], pair_recv.at[it, half], partner,
+            )
+            begin(handed)
+            term = product(q, 1, half)
+            handed.wait_recv()
+            acc[1, place, :] += term + from_partner[it, half]
+            for g in ((3, 2) if half is far else (1, 0)):
+                for col in (both, second):
+                    begin(scatter(0, order[g], col, to_second))
+
+        def add(stage_, plane, col):
+            which = at(plane, col)
+            scatter(stage_, plane, col, partner).wait_recv()
+            acc[1, piece(which), :] += received[it, stage_, which]
+
+        for g in (3, 2, 1, 0):
+            add(0, order[g], first)
+            begin(scatter(1, order[g], first, to_first))
+            add(0, order[g], self_)
+        for g in (3, 2, 1):
+            add(1, order[g], self_)
+            begin(to_plane(order[g], z))
+        add(1, z, self_)
+        summed = acc[1, piece(chip), :]
+        for g in (1, 2, 3):
+            to_plane(order[g], order[g]).wait_recv()
+            summed = summed + received[it, 2, order[g]]
         mine = (source[...] - summed) / gap
         if it + 1 < ITERS:
             gathered[it + 1, own] = mine
@@ -225,7 +262,7 @@
         else:
             out[...] = mine
             later = []
-        for copy in sends + handed + scattered:
+        for copy in sends:
             copy.wait_send()
         sends = later
 
@@ -255,14 +292,14 @@
             pltpu.VMEM((2, chips * rows, width), F32),
             pltpu.VMEM((ITERS, 2 * chips, rows, width), F32),
             pltpu.VMEM((ITERS, HALVES, tall, width), F32),
-            pltpu.VMEM((ITERS, chips, rows, width), F32),
+            pltpu.VMEM((ITERS, 3, chips, rows, width), F32),
             dma((2, terms)),
-            dma((ITERS, 2, chips)),
+            dma((ITERS, 4, chips)),
             dma((ITERS, 2 * chips)),
             dma((ITERS, HALVES)),
             dma((ITERS, HALVES)),
-            dma((ITERS, chips)),
-            dma((ITERS, chips)),
+            dma((ITERS, 3, chips)),
+            dma((ITERS, 3, chips)),
         ],
         compiler_params=pltpu.CompilerParams(collective_id=0, has_side_effects=True),
     )(
@@ -293,8 +330,8 @@
     rows, width = source.shape
     whole = chips * 2 * rows
     fits = (
-        rows % 16 == 0 and sizes[1] % 2 == 0 and GROUPS == 4 and chips % GROUPS == 0
-        and HALVES == 2 and whole % (GROUPS * 128) == 0 and width % 128 == 0
+        rows % 16 == 0 and sizes == (2 * GROUPS, 4) and GROUPS == 4 and HALVES == 2
+        and whole % (GROUPS * 128) == 0 and width % 128 == 0
     )
     return fused(sizes, source, *rest) if fits else plain(source, *rest)
 

time: 76.6 us -> 71.3 us (0.931)
  Pallas kernels: 75 us -> 69.8 us
    pallas_call x1, Pallas kernels: 75 us -> 69.8 us  [fused(): pl.pallas_call(functools.partial(kernel, (naux, ngrp, rows)), out_shape=j...]
where the time goes in v2:
time: 71.3 us; the launch traced here: 71.1 us
  Pallas kernels  69.8 us (98%)
  local copies, waits for them, and re-layouts  1.38 us (2%)
    pallas_call x1, Pallas kernels, fused(): pl.pallas_call(functools.partial(kernel, (naux, ngrp, rows)), out_shape=j...  69.8 us

profile of v2, /device:TPU:0, one launch (start us, length us, event | category | flops | bytes accessed | tf_op | source)
XLA Modules:
  0.0 71.1 jit_solution(1058413571579462464)
XLA Ops:
  0.0 69.8 %shard_map.55 = f32[32,256]{1,0:T(8,128)} custom-call(f32[32,256]{1,0:T(8,128)} %source.1, f32[1,32]{1,0:T(1,128)} %bitcast.5, f32[1,256]{1,0:T(1,128)} %bitcast.4, f32[2,256,256]{2,1,0:T(8,128)} %oo.1, f32[2,16,2,32,1024]{4,3,2,1,0:T(8,128)} %bitcast.3), custom_call_target="tpu_custom_call" | custom-call | tf_op jit(solution)/shard_map/pallas_call | solution.py:279
  69.8 1.4 %copy.7 = f32[32,256]{1,0:T(8,128)} copy(f32[32,256]{1,0:T(8,128)} %shard_map.55) | data formatting | bytes 65536

commit v3 on v2

--- a/solution.py
+++ b/solution.py
@@ -57,7 +57,7 @@
         return plane * 4 + col
 
     partner = device(chip, 1 - core)
-    to_first, to_second = device(at(z, first), core), device(at(z, second), core)
+    to_first, to_second, to_both = [device(at(z, col), core) for col in (first, second, both)]
 
     loads = []
     for slot in range(2):
@@ -70,7 +70,7 @@
     barrier = pltpu.get_barrier_semaphore()
     pl.semaphore_signal(barrier, inc=1, device_id=partner, device_id_type=MESH)
     order = [z, z + 1 - 2 * (z % 2), 2 - z // 2, 3 - 3 * (z // 2)]
-    greeted = [to_first, to_second] + [device(at(plane, self_), core) for plane in order[1:]]
+    greeted = [to_first, to_second, to_both] + [device(at(plane, self_), core) for plane in order[1:]]
     for other in greeted:
         pl.semaphore_signal(barrier, inc=1, device_id=other, device_id_type=MESH)
 
@@ -103,13 +103,15 @@
             sends.append(block_copy(it, 2 * which + core, kind, which, target))
             sends[-1].start()
 
+    everyone = ((4, to_both), (0, to_first), (1, to_second), (2, partner))
+
     def start_gather(it):
         sends = []
         for plane in order[1:]:
             there = at(plane, self_)
             sends.append(block_copy(it, own, 3, there, device(there, core)))
             sends[-1].start()
-        pass_on(it, chip, sends, ((0, to_first), (1, to_second), (2, partner)))
+        pass_on(it, chip, sends, everyone)
         return sends
 
     def product(q, slot, half):
@@ -152,15 +154,10 @@
         def from_plane(g):
             which = at(order[g], self_)
             arrived(it, which, core)
-            pass_on(it, which, sends, ((0, to_first), (1, to_second), (2, partner)))
-
-        def from_first(g):
-            which = at(order[g], first)
-            arrived(it, which, core)
-            pass_on(it, which, sends, ((1, to_second), (2, partner)))
-
-        def from_second(g):
-            for col in (second, both):
+            pass_on(it, which, sends, everyone)
+
+        def from_near(g):
+            for col in (first, second, both):
                 which = at(order[g], col)
                 arrived(it, which, core)
                 pass_on(it, which, sends, ((2, partner),))
@@ -187,19 +184,15 @@
             lax.fori_loop(0, 2 * HALVES, step, 0)
 
         from_plane(1)
-        from_first(0)
+        from_near(0)
         from_plane(2)
-        from_first(1)
-        from_second(0)
         from_plane(3)
-        from_first(2)
+        from_near(1)
         accumulate(0)
-        from_first(3)
-        from_second(1)
+        from_near(2)
         accumulate(1)
-        from_second(2)
+        from_near(3)
         accumulate(2)
-        from_second(3)
         q = consume(3)
 
         def piece(which):
@@ -214,8 +207,8 @@
 
         def to_plane(plane, sender):
             return remote(
-                acc.at[1, piece(at(plane, self_))], received.at[it, 2, sender],
-                scatter_send.at[it, 2, plane], scatter_recv.at[it, 2, sender],
+                acc.at[1, piece(at(plane, self_))], received.at[it, 3, sender],
+                scatter_send.at[it, 3, plane], scatter_recv.at[it, 3, sender],
                 device(at(plane, self_), core),
             )
 
@@ -235,26 +228,26 @@
             handed.wait_recv()
             acc[1, place, :] += term + from_partner[it, half]
             for g in ((3, 2) if half is far else (1, 0)):
-                for col in (both, second):
-                    begin(scatter(0, order[g], col, to_second))
-
-        def add(stage_, plane, col):
-            which = at(plane, col)
-            scatter(stage_, plane, col, partner).wait_recv()
-            acc[1, piece(which), :] += received[it, stage_, which]
-
-        for g in (3, 2, 1, 0):
-            add(0, order[g], first)
-            begin(scatter(1, order[g], first, to_first))
-            add(0, order[g], self_)
+                for kind, (col, target) in enumerate(
+                    ((both, to_both), (first, to_first), (second, to_second))
+                ):
+                    begin(scatter(kind, order[g], col, target))
+
+        def reduced(plane):
+            which = at(plane, self_)
+            value = acc[1, piece(which), :]
+            for kind in (1, 2, 0):
+                scatter(kind, plane, self_, partner).wait_recv()
+                value = value + received[it, kind, which]
+            return value
+
         for g in (3, 2, 1):
-            add(1, order[g], self_)
+            acc[1, piece(at(order[g], self_)), :] = reduced(order[g])
             begin(to_plane(order[g], z))
-        add(1, z, self_)
-        summed = acc[1, piece(chip), :]
+        summed = reduced(z)
         for g in (1, 2, 3):
             to_plane(order[g], order[g]).wait_recv()
-            summed = summed + received[it, 2, order[g]]
+            summed = summed + received[it, 3, order[g]]
         mine = (source[...] - summed) / gap
         if it + 1 < ITERS:
             gathered[it + 1, own] = mine
@@ -292,14 +285,14 @@
             pltpu.VMEM((2, chips * rows, width), F32),
             pltpu.VMEM((ITERS, 2 * chips, rows, width), F32),
             pltpu.VMEM((ITERS, HALVES, tall, width), F32),
-            pltpu.VMEM((ITERS, 3, chips, rows, width), F32),
+            pltpu.VMEM((ITERS, 4, chips, rows, width), F32),
             dma((2, terms)),
-            dma((ITERS, 4, chips)),
+            dma((ITERS, 5, chips)),
             dma((ITERS, 2 * chips)),
             dma((ITERS, HALVES)),
             dma((ITERS, HALVES)),
-            dma((ITERS, 3, chips)),
-            dma((ITERS, 3, chips)),
+            dma((ITERS, 4, chips)),
+            dma((ITERS, 4, chips)),
         ],
         compiler_params=pltpu.CompilerParams(collective_id=0, has_side_effects=True),
     )(

time: 71.3 us -> 61.3 us (0.86)
  Pallas kernels: 69.8 us -> 59.7 us
    pallas_call x1, Pallas kernels: 69.8 us -> 59.7 us  [fused(): pl.pallas_call(functools.partial(kernel, (naux, ngrp, rows)), out_shape=j...]
where the time goes in v3:
time: 61.3 us; the launch traced here: 61.1 us
  Pallas kernels  59.7 us (97%)
  local copies, waits for them, and re-layouts  1.38 us (2%)
    pallas_call x1, Pallas kernels, fused(): pl.pallas_call(functools.partial(kernel, (naux, ngrp, rows)), out_shape=j...  59.7 us
    unnamed x1, local copies, waits for them, and re-layouts  1.38 us

profile of v3, /device:TPU:0, one launch (start us, length us, event | category | flops | bytes accessed | tf_op | source)
XLA Modules:
  0.0 61.1 jit_solution(3949261446678081843)
XLA Ops:
  0.0 59.7 %shard_map.55 = f32[32,256]{1,0:T(8,128)} custom-call(f32[32,256]{1,0:T(8,128)} %source.1, f32[1,32]{1,0:T(1,128)} %bitcast.5, f32[1,256]{1,0:T(1,128)} %bitcast.4, f32[2,256,256]{2,1,0:T(8,128)} %oo.1, f32[2,16,2,32,1024]{4,3,2,1,0:T(8,128)} %bitcast.3), custom_call_target="tpu_custom_call" | custom-call | tf_op jit(solution)/shard_map/pallas_call | solution.py:272
  59.7 1.4 %copy.7 = f32[32,256]{1,0:T(8,128)} copy(f32[32,256]{1,0:T(8,128)} %shard_map.55) | data formatting | bytes 65536

commit v4 on v3

--- a/solution.py
+++ b/solution.py
@@ -186,9 +186,9 @@
         from_plane(1)
         from_near(0)
         from_plane(2)
+        accumulate(0)
         from_plane(3)
         from_near(1)
-        accumulate(0)
         from_near(2)
         accumulate(1)
         from_near(3)

time: 61.3 us -> 60.9 us (level)
  no operation moved by 1% of the time
where the time goes in v4:
time: 60.9 us; the launch traced here: 60.7 us
  Pallas kernels  59.3 us (97%)
  local copies, waits for them, and re-layouts  1.38 us (2%)
    pallas_call x1, Pallas kernels, fused(): pl.pallas_call(functools.partial(kernel, (naux, ngrp, rows)), out_shape=j...  59.3 us
    unnamed x1, local copies, waits for them, and re-layouts  1.38 us

profile of v4, /device:TPU:0, one launch (start us, length us, event | category | flops | bytes accessed | tf_op | source)
XLA Modules:
  0.0 60.7 jit_solution(5025684913852652391)
XLA Ops:
  0.0 59.3 %shard_map.55 = f32[32,256]{1,0:T(8,128)} custom-call(f32[32,256]{1,0:T(8,128)} %source.1, f32[1,32]{1,0:T(1,128)} %bitcast.5, f32[1,256]{1,0:T(1,128)} %bitcast.4, f32[2,256,256]{2,1,0:T(8,128)} %oo.1, f32[2,16,2,32,1024]{4,3,2,1,0:T(8,128)} %bitcast.3), custom_call_target="tpu_custom_call" | custom-call | tf_op jit(solution)/shard_map/pallas_call | solution.py:272
  59.3 1.4 %copy.7 = f32[32,256]{1,0:T(8,128)} copy(f32[32,256]{1,0:T(8,128)} %shard_map.55) | data formatting | bytes 65536
